TPU v7x, 256 devices: a whole 4x4x8 slice. The times are simulated.
256 devices in a mesh: seq: 32 (over z, y_lo, core), head: 8 (over y_hi, x).
Axes of the slice: x: 4, y: 4 (y_hi: 2, y_lo: 2; y = y_hi * 2 + y_lo), z: 8, core: 2. Of those that a mesh axis runs over, the one named last changes fastest.
Arguments:
- normed_layer_input: bfloat16 [8192, 8192], P('seq', 'head'), may hold values from -6 to 6
- query_projection_input: bfloat16 [8192, 8192], P('seq', 'head'), may hold values from -9 to 9, as said below
- key_projection_input: bfloat16 [8192, 1024], P('seq', 'head'), may hold values from -9 to 9, as said below
- value_projection_input: bfloat16 [8192, 1024], P('seq', 'head'), may hold values from -6 to 6
- output_gradient: bfloat16 [8192, 8192], P('seq', 'head'), may hold values from -12 to 12
- adapter_down_weight: bfloat16 [3, 8, 8192], P(None, None, 'head'), may hold values from -0.0007324219 to 0.0007324219
- adapter_up_query: bfloat16 [8, 8192], P(None, 'head'), may hold values from -0.0007324219 to 0.0007324219
- adapter_up_kv: bfloat16 [2, 8, 1024], P(None, None, 'head'), may hold values from -0.001953125 to 0.001953125
Outputs:
- query_projection_gradient: bfloat16 [8192, 8192], P('seq', 'head')
- key_projection_gradient: bfloat16 [8192, 1024], P('seq', 'head')
- value_projection_gradient: bfloat16 [8192, 1024], P('seq', 'head')
- adapter_down_gradient: float32 [3, 8, 8192], P(None, None, 'head')
- adapter_up_query_gradient: float32 [8, 8192], P(None, 'head')
- adapter_up_kv_gradient: float32 [2, 8, 1024], P(None, None, 'head')
Inputs may be any that keep to these rules, and one draw needn't show every extreme that they name: `query_projection_input`: real values. `key_projection_input`: real values.
All inputs are finite; a program needn't handle non-finite values.
Results may differ from a plain program's by a relative error of at most 0.029.
Values may be sent and summed in bfloat16 or wider, within the bound.
A program may use at most 64 MiB of HBM per device.

v0:
```python
import jax
import jax.numpy as jnp
from jax import lax
from jax.sharding import PartitionSpec as P

HEAD_SIZE = 128
position_scale = 0.04096


def from_behind(value, axis, steps):
    count = lax.axis_size(axis)
    pairs = [(source, (source + steps) % count) for source in range(count)]
    return lax.ppermute(value, axis, pairs)


def rope_tables(positions, feature_count):
    half_width = feature_count // 2
    frequency = position_scale * 10000.0 ** (
        -2.0 * jnp.arange(half_width, dtype=jnp.float32) / feature_count
    )
    angles = positions.astype(jnp.float32)[:, None] * frequency[None, :]
    return (jnp.cos(angles)[:, None, :], jnp.sin(angles)[:, None, :])


def rotate(vectors, cosine_table, sine_table):
    half_width = vectors.shape[-1] // 2
    low_half = vectors[..., :half_width]
    high_half = vectors[..., half_width:]
    return jnp.concatenate(
        [
            low_half * cosine_table - high_half * sine_table,
            high_half * cosine_table + low_half * sine_table,
        ],
        axis=-1,
    )


def unrotate(gradient, cosine_table, sine_table):
    half_width = gradient.shape[-1] // 2
    low_half = gradient[..., :half_width]
    high_half = gradient[..., half_width:]
    return jnp.concatenate(
        [
            low_half * cosine_table + high_half * sine_table,
            high_half * cosine_table - low_half * sine_table,
        ],
        axis=-1,
    )


def body(
    normed_layer_input,
    query_projection_input,
    key_projection_input,
    value_projection_input,
    output_gradient,
    adapter_down_weight,
    adapter_up_query,
    adapter_up_kv,
):
    tok_rows = query_projection_input.shape[0]
    query_count = query_projection_input.shape[1] // HEAD_SIZE
    query_width = query_count * HEAD_SIZE
    seq_count = lax.axis_size("seq")
    head_axis_count = lax.axis_size("head")
    group_dev = seq_count // 4
    half_offset = seq_count // 8
    seq_index = lax.axis_index("seq")
    shifted = lax.axis_index("head") >= head_axis_count // 2
    group_place = jnp.where(shifted, (seq_index - half_offset) % seq_count, seq_index) % group_dev
    positions = seq_index * tok_rows + jnp.arange(tok_rows, dtype=jnp.int32)
    cosine_table, sine_table = rope_tables(positions, HEAD_SIZE)
    query_rot = rotate(
        query_projection_input.astype(jnp.float32).reshape(tok_rows, query_count, HEAD_SIZE),
        cosine_table,
        sine_table,
    ).astype(jnp.bfloat16)
    key_rot = (
        rotate(
            key_projection_input.astype(jnp.float32).reshape(tok_rows, 1, HEAD_SIZE),
            cosine_table,
            sine_table,
        )
        .astype(jnp.bfloat16)
        .reshape(tok_rows, HEAD_SIZE)
    )
    grad_heads = output_gradient.reshape(tok_rows, query_count, HEAD_SIZE)
    key_value = jnp.concatenate([key_rot, value_projection_input], axis=1)
    block_list = [key_value]
    moving = key_value
    for cycle_step in range(group_dev - 1):
        moving = from_behind(moving, "seq", 1)
        block_list.append(moving)
    blocks = jnp.stack(block_list)
    key_all = blocks[:, :, :HEAD_SIZE].reshape(group_dev * tok_rows, HEAD_SIZE)
    value_all = blocks[:, :, HEAD_SIZE:].reshape(group_dev * tok_rows, HEAD_SIZE)
    score_scale = HEAD_SIZE ** (-0.5)
    query_pos = jnp.arange(tok_rows, dtype=jnp.int32)[:, None]
    column = jnp.arange(group_dev * tok_rows, dtype=jnp.int32)[None, :]
    source_block = column // tok_rows
    allowed = (group_place >= source_block) & (
        (source_block > 0) | (column % tok_rows <= query_pos)
    )
    heads_step = max(1, min(query_count, 512 // tok_rows))
    while query_count % heads_step != 0:
        heads_step = heads_step - 1
    step_count = query_count // heads_step
    query_steps = query_rot.reshape(tok_rows, step_count, heads_step, HEAD_SIZE).transpose(
        1, 0, 2, 3
    )
    grad_steps = grad_heads.reshape(tok_rows, step_count, heads_step, HEAD_SIZE).transpose(
        1, 0, 2, 3
    )

    def head_block(operands):
        query_blk, grad_blk = operands
        scores = (
            jnp.einsum("qhd,kd->hqk", query_blk, key_all, preferred_element_type=jnp.float32)
            * score_scale
        )
        masked = jnp.where(allowed, scores, -jnp.inf)
        row_top = jnp.max(masked, axis=-1, keepdims=True)
        log_total = row_top + jnp.log(jnp.sum(jnp.exp(masked - row_top), axis=-1, keepdims=True))
        weights = jnp.where(allowed, jnp.exp(scores - log_total), 0.0)
        prob_bf16 = weights.astype(jnp.bfloat16)
        attn_out = jnp.einsum(
            "hqk,kd->qhd", prob_bf16, value_all, preferred_element_type=jnp.float32
        ).astype(jnp.bfloat16)
        row_delta = jnp.sum(attn_out.astype(jnp.float32) * grad_blk.astype(jnp.float32), axis=-1).T[
            :, :, None
        ]
        prob_grad = jnp.einsum(
            "qhd,kd->hqk", grad_blk, value_all, preferred_element_type=jnp.float32
        )
        dscore = (weights * (prob_grad - row_delta)).astype(jnp.bfloat16)
        query_part = (
            jnp.einsum("hqk,kd->qhd", dscore, key_all, preferred_element_type=jnp.float32)
            * score_scale
        )
        key_part = (
            jnp.einsum("hqk,qhd->kd", dscore, query_blk, preferred_element_type=jnp.float32)
            * score_scale
        )
        value_part = jnp.einsum(
            "hqk,qhd->kd", prob_bf16, grad_blk, preferred_element_type=jnp.float32
        )
        return (query_part, key_part, value_part, log_total[:, :, 0], row_delta[:, :, 0])

    results = lax.map(head_block, (query_steps, grad_steps))
    query_rot_grad = results[0].transpose(1, 0, 2, 3).reshape(tok_rows, query_count, HEAD_SIZE)
    key_terms = jnp.sum(results[1], axis=0)
    value_terms = jnp.sum(results[2], axis=0)
    block_terms = jnp.stack(
        [
            key_terms.reshape(group_dev, tok_rows, HEAD_SIZE),
            value_terms.reshape(group_dev, tok_rows, HEAD_SIZE),
        ],
        axis=1,
    )
    carried = block_terms[group_dev - 1]
    for offset_back in range(group_dev - 2, -1, -1):
        carried = (
            from_behind(carried.astype(jnp.bfloat16), "seq", -1).astype(carried.dtype)
            + block_terms[offset_back]
        )
    query_gradient = (
        unrotate(query_rot_grad, cosine_table, sine_table)
        .astype(jnp.bfloat16)
        .reshape(tok_rows, query_width)
    )
    key_gradient = (
        unrotate(carried[0].reshape(tok_rows, 1, HEAD_SIZE), cosine_table, sine_table)
        .astype(jnp.bfloat16)
        .reshape(tok_rows, HEAD_SIZE)
    )
    value_gradient = carried[1].astype(jnp.bfloat16)
    kv_pile = jnp.stack([key_gradient, value_gradient])
    down_piece = jnp.einsum(
        "zg,wfg->zwf", normed_layer_input, adapter_down_weight, preferred_element_type=jnp.float32
    )
    back_query = jnp.dot(query_gradient, adapter_up_query.T, preferred_element_type=jnp.float32)
    back_pair = jnp.einsum(
        "xfn,xqn->fxq", kv_pile, adapter_up_kv, preferred_element_type=jnp.float32
    )
    backward_piece = jnp.concatenate([back_query[:, None, :], back_pair], axis=1)
    down_sum, back_sum = (
        lax.psum(down_piece.astype(jnp.bfloat16), "head").astype(jnp.float32),
        lax.psum(backward_piece.astype(jnp.bfloat16), "head").astype(jnp.float32),
    )
    down_activation = down_sum.astype(jnp.bfloat16)
    backward_activation = back_sum.astype(jnp.bfloat16)
    up_query_local = 2.0 * jnp.einsum(
        "yj,yq->jq", down_activation[:, 0], query_gradient, preferred_element_type=jnp.float32
    )
    up_pair_local = 2.0 * jnp.einsum(
        "yij,iyq->ijq", down_activation[:, 1:], kv_pile, preferred_element_type=jnp.float32
    )
    down_local = 2.0 * jnp.einsum(
        "yhu,ym->hum", backward_activation, normed_layer_input, preferred_element_type=jnp.float32
    )
    down_total, up_query_total, up_pair_total = (
        lax.psum(down_local.astype(jnp.bfloat16), "seq").astype(jnp.float32),
        lax.psum(up_query_local.astype(jnp.bfloat16), "seq").astype(jnp.float32),
        lax.psum(up_pair_local.astype(jnp.bfloat16), "seq").astype(jnp.float32),
    )
    return (query_gradient, key_gradient, value_gradient, down_total, up_query_total, up_pair_total)


def solution(mesh):
    placed = (
        P("seq", "head"),
        P("seq", "head"),
        P("seq", "head"),
        P("seq", "head"),
        P("seq", "head"),
        P(None, None, "head"),
        P(None, "head"),
        P(None, None, "head"),
    )
    return jax.shard_map(
        body,
        mesh=mesh,
        in_specs=placed,
        out_specs=(
            P("seq", "head"),
            P("seq", "head"),
            P("seq", "head"),
            P(None, None, "head"),
            P(None, "head"),
            P(None, None, "head"),
        ),
        check_vma=False,
    )
```

profile of v0, /device:TPU:41, one launch (start us, length us, event | category | flops | bytes accessed | tf_op | source)
XLA Modules:
  0.0 416.2 jit_solution(2638873507155498322)
XLA Ops:
  10.4 2.1 collective-permute-start
  17.0 2.0 copy.29
  21.7 3.2 collective-permute-start.2
  26.8 3.3 collective-permute-start.3
  32.1 3.3 collective-permute-start.4
  37.4 3.3 collective-permute-start.5
  42.7 3.3 collective-permute-start.6
  51.0 56.7 %while.15 = (s32[]{:T(128)}, f32[4,256,2,128]{3,1,2,0:T(8,128)S(1)}, f32[4,2048,128]{2,1,0:T(8,128)}, f32[4,2048,128]{2,1,0:T(8,128)}, bf16[4,256,2,128]{3,1,2,0...) while((s32[]{:T(128)}, ...), condition=%wide.region_4.5_spmd.clone, body=%wide.region_0.4_spmd.clone.sunk | while | flops 1634860032 | bytes 71749384 | solution.py:149
  54.9 2.3 fusion.144
  57.3 3.7 fusion.140
  62.7 1.8 fusion.143
  69.1 2.3 fusion.144
  71.5 3.7 fusion.140
  75.2 1.7 fusion.141
  76.9 1.7 fusion.143
  83.2 2.3 fusion.144
  85.6 3.7 fusion.140
  91.0 1.7 fusion.143
  97.3 2.4 fusion.144
  99.9 3.7 fusion.140
  105.2 1.7 fusion.143
  107.7 2.8 reduce_sum.36
  110.6 2.5 reduce_sum.37
  113.2 6.0 %collective-permute-done.7 = bf16[2,256,128]{2,1,0:T(8,128)(2,1)S(1)} collective-permute-done((bf16[2,256,128]{2,1,0:T(8,128)(2,1)S(1)}, bf16[2,256,128]{2,1,0:T(8,128)(2,1)S(1)}, u32[]{:S(2)}, u32[]{:S(2)}) %collective-permute-start.7) | collective-permute-done | bytes 131104 | tf_op jit(solution)/shard_map/ppermute | solution.py:13
  119.3 5.3 %collective-permute-done.8 = bf16[2,256,128]{2,1,0:T(8,128)(2,1)S(1)} collective-permute-done((bf16[2,256,128]{2,1,0:T(8,128)(2,1)S(1)}, bf16[2,256,128]{2,1,0:T(8,128)(2,1)S(1)}, u32[]{:S(2)}, u32[]{:S(2)}) %collective-permute-start.8) | collective-permute-done | bytes 131104 | tf_op jit(solution)/shard_map/ppermute | solution.py:13
  124.7 5.3 %collective-permute-done.9 = bf16[2,256,128]{2,1,0:T(8,128)(2,1)S(1)} collective-permute-done((bf16[2,256,128]{2,1,0:T(8,128)(2,1)S(1)}, bf16[2,256,128]{2,1,0:T(8,128)(2,1)S(1)}, u32[]{:S(2)}, u32[]{:S(2)}) %collective-permute-start.9) | collective-permute-done | bytes 131104 | tf_op jit(solution)/shard_map/ppermute | solution.py:13
  130.6 5.0 %collective-permute-done.10 = bf16[2,256,128]{2,1,0:T(8,128)(2,1)S(1)} collective-permute-done((bf16[2,256,128]{2,1,0:T(8,128)(2,1)S(1)}, bf16[2,256,128]{2,1,0:T(8,128)(2,1)S(1)}, u32[]{:S(2)}, u32[]{:S(2)}) %collective-permute-start.10) | collective-permute-done | bytes 131104 | tf_op jit(solution)/shard_map/ppermute | solution.py:13
  136.1 4.9 %collective-permute-done.11 = bf16[2,256,128]{2,1,0:T(8,128)(2,1)S(1)} collective-permute-done((bf16[2,256,128]{2,1,0:T(8,128)(2,1)S(1)}, bf16[2,256,128]{2,1,0:T(8,128)(2,1)S(1)}, u32[]{:S(2)}, u32[]{:S(2)}) %collective-permute-start.11) | collective-permute-done | bytes 131104 | tf_op jit(solution)/shard_map/ppermute | solution.py:13
  143.0 3.4 collective-permute-done.12
  146.8 5.0 %collective-permute-done.13 = bf16[2,256,128]{2,1,0:T(8,128)(2,1)S(1)} collective-permute-done((bf16[2,256,128]{2,1,0:T(8,128)(2,1)S(1)}, bf16[2,256,128]{2,1,0:T(8,128)(2,1)S(1)}, u32[]{:S(2)}, u32[]{:S(2)}) %collective-permute-start.13) | collective-permute-done | bytes 131104 | tf_op jit(solution)/shard_map/ppermute | solution.py:13
  152.8 34.4 %all-reduce.1 = (bf16[256,3,8]{0,2,1:T(8,128)(2,1)S(1)}, bf16[256,3,8]{0,2,1:T(8,128)(2,1)S(1)}) all-reduce(bf16[256,3,8]{0,2,1:T(8,128)(2,1)S(1)} %pad_maximum_fusion.6, bf16[256,3,8]{0,2,1:T(8,128)(2,1)S(1)} %convolution_convert_fusion.1), channel_id=1, replica_groups=mesh['seq'=32,'head'=8] {'head'}, use_global_device_ids=true, to_apply=%region_7.8 | all-reduce | flops 12288 | bytes 49152 | tf_op jit(solution)/shard_map/psum | solution.py:188
  190.9 214.4 %all-reduce.4.cloned.1.call-done = (bf16[3,8,1024]{2,1,0:T(8,128)(2,1)}, bf16[8,1024]{1,0:T(8,128)(2,1)}, bf16[2,8,128]{2,1,0:T(8,128)(2,1)}) async-done(((bf16[3,8,1024]{2,1,0:T(8,128)(2,1)}, bf16[8,1024]{1,0:T(8,128)(2,1)}, bf16[2,8,128]{2,1,0:T(8,128)(2,1)}), (bf16[3,8,1024]{2,1,0:T(8,128)(2,1)}, bf16[8,1024]{1,0:T(8,128)(2,1)}, bf16[2,8,128]{2,1,0:T(8,128)(2,1)})) %all-reduce.4.cloned.1.call-update) | async-done | bytes 69648 | tf_op jit(solution)/shard_map/psum | solution.py:202
  (167 shorter events, 58.8 us)
Async XLA Ops:
  7.2 123.2 %copy-start = (bf16[256,1024]{1,0:T(8,128)(2,1)S(1)}, bf16[256,1024]{1,0:T(8,128)(2,1)}, u32[]{:S(2)}) copy-start(bf16[256,1024]{1,0:T(8,128)(2,1)} %param.10) | copy-start | bytes 1572868
  7.2 398.1 %all-reduce.4.cloned.1.call-start = ((), (), s32[]{:S(2)}) async-start(), calls=%async_computation | async-start | bytes 139264 | tf_op jit(solution)/shard_map/psum | solution.py:202
  7.2 8.5 %copy-start.15 = (f32[64]{0:T(128)}, f32[64]{0:T(128)S(1)}, u32[]{:S(2)}) copy-start(f32[64]{0:T(128)S(1)} %power_multiply_fusion) | copy-start | bytes 772
  7.3 8.4 %copy-start.13 = (f32[256]{0:T(256)}, f32[256]{0:T(256)S(1)}, u32[]{:S(2)}) copy-start(f32[256]{0:T(256)S(1)} %add_convert_fusion.1) | copy-start | bytes 3076
  10.4 8.9 %collective-permute-start = (bf16[256,256]{1,0:T(8,128)(2,1)S(1)}, bf16[256,256]{1,0:T(8,128)(2,1)}, u32[]{:S(2)}, u32[]{:S(2)}) collective-permute-start(bf16[256,256]{1,0:T(8,128)(2,1)S(1)} %get-tuple-element.124), channel_id=1, source_target_pairs={{0,8},{8,16},{16,24},{24,32},{32,40},{40,48},{48,56},{56,64},{64,7... | collective-permute-start | bytes 393224 | tf_op jit(solution)/shard_map/ppermute | solution.py:13
  13.0 3.9 copy-start.6
  19.3 2.3 collective-permute-start.1
  21.7 5.2 %collective-permute-start.2 = (bf16[256,256]{1,0:T(8,128)(2,1)S(1)}, bf16[256,256]{1,0:T(8,128)(2,1)S(1)}, u32[]{:S(2)}, u32[]{:S(2)}) collective-permute-start(bf16[256,256]{1,0:T(8,128)(2,1)S(1)} %collective-permute-done.1), channel_id=1, source_target_pairs={{0,8},{8,16},{16,24},{24,32},{32,40},{40,48},{48,56},{56,64},{64,7... | collective-permute-start | bytes 393224 | tf_op jit(solution)/shard_map/ppermute | solution.py:13
  26.8 5.3 %collective-permute-start.3 = (bf16[256,256]{1,0:T(8,128)(2,1)S(1)}, bf16[256,256]{1,0:T(8,128)(2,1)S(1)}, u32[]{:S(2)}, u32[]{:S(2)}) collective-permute-start(bf16[256,256]{1,0:T(8,128)(2,1)S(1)} %collective-permute-done.2), channel_id=1, source_target_pairs={{0,8},{8,16},{16,24},{24,32},{32,40},{40,48},{48,56},{56,64},{64,7... | collective-permute-start | bytes 393224 | tf_op jit(solution)/shard_map/ppermute | solution.py:13
  32.1 5.3 %collective-permute-start.4 = (bf16[256,256]{1,0:T(8,128)(2,1)S(1)}, bf16[256,256]{1,0:T(8,128)(2,1)S(1)}, u32[]{:S(2)}, u32[]{:S(2)}) collective-permute-start(bf16[256,256]{1,0:T(8,128)(2,1)S(1)} %collective-permute-done.3), channel_id=1, source_target_pairs={{0,8},{8,16},{16,24},{24,32},{32,40},{40,48},{48,56},{56,64},{64,7... | collective-permute-start | bytes 393224 | tf_op jit(solution)/shard_map/ppermute | solution.py:13
  37.4 5.3 %collective-permute-start.5 = (bf16[256,256]{1,0:T(8,128)(2,1)S(1)}, bf16[256,256]{1,0:T(8,128)(2,1)S(1)}, u32[]{:S(2)}, u32[]{:S(2)}) collective-permute-start(bf16[256,256]{1,0:T(8,128)(2,1)S(1)} %collective-permute-done.4), channel_id=1, source_target_pairs={{0,8},{8,16},{16,24},{24,32},{32,40},{40,48},{48,56},{56,64},{64,7... | collective-permute-start | bytes 393224 | tf_op jit(solution)/shard_map/ppermute | solution.py:13
  42.7 5.3 %collective-permute-start.6 = (bf16[256,256]{1,0:T(8,128)(2,1)S(1)}, bf16[256,256]{1,0:T(8,128)(2,1)S(1)}, u32[]{:S(2)}, u32[]{:S(2)}) collective-permute-start(bf16[256,256]{1,0:T(8,128)(2,1)S(1)} %collective-permute-done.5), channel_id=1, source_target_pairs={{0,8},{8,16},{16,24},{24,32},{32,40},{40,48},{48,56},{56,64},{64,7... | collective-permute-start | bytes 393224 | tf_op jit(solution)/shard_map/ppermute | solution.py:13
  57.3 3.7 copy-start.2
  57.3 3.7 copy-start.8
  71.5 3.7 copy-start.8
  85.6 3.7 copy-start.8
  99.9 3.7 copy-start.8
  113.1 17.3 %copy-start.11 = (bf16[3,8,1024]{2,1,0:T(8,128)(2,1)S(1)}, bf16[3,8,1024]{2,1,0:T(8,128)(2,1)}, u32[]{:S(2)}) copy-start(bf16[3,8,1024]{2,1,0:T(8,128)(2,1)} %param.15) | copy-start | bytes 147460
  113.1 6.1 %collective-permute-start.7 = (bf16[2,256,128]{2,1,0:T(8,128)(2,1)S(1)}, bf16[2,256,128]{2,1,0:T(8,128)(2,1)S(1)}, u32[]{:S(2)}, u32[]{:S(2)}) collective-permute-start(bf16[2,256,128]{2,1,0:T(8,128)(2,1)S(1)} %fusion.86), channel_id=1, source_target_pairs={{0,248},{8,0},{16,8},{24,16},{32,24},{40,32},{48,40},{56,48},{64,5... | collective-permute-start | bytes 393224 | tf_op jit(solution)/shard_map/ppermute | solution.py:13
  119.2 16.5 %copy-start.5 = (f32[4,256,2,128]{3,1,2,0:T(8,128)S(1)}, f32[4,256,2,128]{3,1,2,0:T(8,128)}, u32[]{:S(2)}) copy-start(f32[4,256,2,128]{3,1,2,0:T(8,128)} %copy-done.4) | copy-start | bytes 3145732
  119.3 5.4 %collective-permute-start.8 = (bf16[2,256,128]{2,1,0:T(8,128)(2,1)S(1)}, bf16[2,256,128]{2,1,0:T(8,128)(2,1)S(1)}, u32[]{:S(2)}, u32[]{:S(2)}) collective-permute-start(bf16[2,256,128]{2,1,0:T(8,128)(2,1)S(1)} %fusion.51), channel_id=1, source_target_pairs={{0,248},{8,0},{16,8},{24,16},{32,24},{40,32},{48,40},{56,48},{64,5... | collective-permute-start | bytes 393224 | tf_op jit(solution)/shard_map/ppermute | solution.py:13
  124.7 5.4 %collective-permute-start.9 = (bf16[2,256,128]{2,1,0:T(8,128)(2,1)S(1)}, bf16[2,256,128]{2,1,0:T(8,128)(2,1)S(1)}, u32[]{:S(2)}, u32[]{:S(2)}) collective-permute-start(bf16[2,256,128]{2,1,0:T(8,128)(2,1)S(1)} %fusion.55), channel_id=1, source_target_pairs={{0,248},{8,0},{16,8},{24,16},{32,24},{40,32},{48,40},{56,48},{64,5... | collective-permute-start | bytes 393224 | tf_op jit(solution)/shard_map/ppermute | solution.py:13
  130.1 5.6 %collective-permute-start.10 = (bf16[2,256,128]{2,1,0:T(8,128)(2,1)S(1)}, bf16[2,256,128]{2,1,0:T(8,128)(2,1)S(1)}, u32[]{:S(2)}, u32[]{:S(2)}) collective-permute-start(bf16[2,256,128]{2,1,0:T(8,128)(2,1)S(1)} %fusion.59), channel_id=1, source_target_pairs={{0,248},{8,0},{16,8},{24,16},{32,24},{40,32},{48,40},{56,48},{64,5... | collective-permute-start | bytes 393224 | tf_op jit(solution)/shard_map/ppermute | solution.py:13
  130.6 10.5 %copy-start.7 = (f32[256,64]{1,0:T(8,128)S(1)}, f32[256,64]{1,0:T(8,128)}, u32[]{:S(2)}) copy-start(f32[256,64]{1,0:T(8,128)} %copy-done.6) | copy-start | bytes 196612
  135.7 5.4 %collective-permute-start.11 = (bf16[2,256,128]{2,1,0:T(8,128)(2,1)S(1)}, bf16[2,256,128]{2,1,0:T(8,128)(2,1)S(1)}, u32[]{:S(2)}, u32[]{:S(2)}) collective-permute-start(bf16[2,256,128]{2,1,0:T(8,128)(2,1)S(1)} %fusion.63), channel_id=1, source_target_pairs={{0,248},{8,0},{16,8},{24,16},{32,24},{40,32},{48,40},{56,48},{64,5... | collective-permute-start | bytes 393224 | tf_op jit(solution)/shard_map/ppermute | solution.py:13
  141.1 5.4 %collective-permute-start.12 = (bf16[2,256,128]{2,1,0:T(8,128)(2,1)S(1)}, bf16[2,256,128]{2,1,0:T(8,128)(2,1)S(1)}, u32[]{:S(2)}, u32[]{:S(2)}) collective-permute-start(bf16[2,256,128]{2,1,0:T(8,128)(2,1)S(1)} %fusion.67), channel_id=1, source_target_pairs={{0,248},{8,0},{16,8},{24,16},{32,24},{40,32},{48,40},{56,48},{64,5... | collective-permute-start | bytes 393224 | tf_op jit(solution)/shard_map/ppermute | solution.py:13
  141.2 5.4 %copy-start.12 = (bf16[8,1024]{1,0:T(8,128)(2,1)S(1)}, bf16[8,1024]{1,0:T(8,128)(2,1)}, u32[]{:S(2)}) copy-start(bf16[8,1024]{1,0:T(8,128)(2,1)} %param.16) | copy-start | bytes 49156
  142.6 9.4 %copy-start.14 = (f32[256]{0:T(256)S(1)}, f32[256]{0:T(256)}, u32[]{:S(2)}) copy-start(f32[256]{0:T(256)} %copy-done.13) | copy-start | bytes 3076
  142.6 9.4 %copy-start.16 = (f32[64]{0:T(128)S(1)}, f32[64]{0:T(128)}, u32[]{:S(2)}) copy-start(f32[64]{0:T(128)} %copy-done.15) | copy-start | bytes 772
  142.6 9.9 %copy-start.17 = (bf16[2,8,128]{2,1,0:T(8,128)(2,1)S(1)}, bf16[2,8,128]{2,1,0:T(8,128)(2,1)}, u32[]{:S(2)}) copy-start(bf16[2,8,128]{2,1,0:T(8,128)(2,1)} %param.17) | copy-start | bytes 12292
  143.0 47.9 %copy-start.3 = (bf16[32,8,8,128]{3,1,2,0:T(8,128)(2,1)}, bf16[32,8,8,128]{3,1,2,0:T(8,128)(2,1)S(1)}, u32[]{:S(2)}) copy-start(bf16[32,8,8,128]{3,1,2,0:T(8,128)(2,1)S(1)} %copy.50) | copy-start | bytes 1572868
  146.5 5.4 %collective-permute-start.13 = (bf16[2,256,128]{2,1,0:T(8,128)(2,1)S(1)}, bf16[2,256,128]{2,1,0:T(8,128)(2,1)S(1)}, u32[]{:S(2)}, u32[]{:S(2)}) collective-permute-start(bf16[2,256,128]{2,1,0:T(8,128)(2,1)S(1)} %fusion.45), channel_id=1, source_target_pairs={{0,248},{8,0},{16,8},{24,16},{32,24},{40,32},{48,40},{56,48},{64,5... | collective-permute-start | bytes 393224 | tf_op jit(solution)/shard_map/ppermute | solution.py:13
  (16 other events, 42.7 us)
Sparse Core Ops, SparseCore 0:
  190.3 214.9 all-reduce.3
where the time goes:
time: 417 us; the launch traced here: 416 us
  waiting for transfers between devices  256 us (61%)
  matrix products  47.8 us (11%)
  blocking collectives  34.4 us (8%)
  other arithmetic  25.6 us (6%)
  starting transfers between devices  19.6 us (5%)
  local copies, waits for them, and re-layouts  17.4 us (4%)
  between operations  14.5 us (3%)
    psum x1, waiting for transfers between devices, body(): lax.psum(down_local.astype(jnp.bfloat16), 'seq').astype(jnp.float32)  214 us
    ppermute x14, waiting for transfers between devices, from_behind(): return lax.ppermute(value, axis, pairs)  42 us
    psum x1, blocking collectives, body(): lax.psum(backward_piece.astype(jnp.bfloat16), 'head').astype(jnp.float32)  34.4 us
    ppermute x14, starting transfers between devices, from_behind(): return lax.ppermute(value, axis, pairs)  19.6 us
    dot_general x4, matrix products, head_block(): jnp.einsum('hqk,kd->qhd', prob_bf16, value_all, preferred_element_type=jn...  14.7 us
    dot_general x4, matrix products, head_block(): jnp.einsum('hqk,qhd->kd', prob_bf16, grad_blk, preferred_element_type=jnp...  9.35 us
  transfers between devices with their start and end apart: 15, of which 14 were waited for; matrix products, arithmetic and copies ran while one was open for 4% of the time, Pallas kernels for 0%

commit v1 on v0

--- a/solution.py
+++ b/solution.py
@@ -199,7 +199,7 @@
         "yhu,ym->hum", backward_activation, normed_layer_input, preferred_element_type=jnp.float32
     )
     down_total, up_query_total, up_pair_total = (
-        lax.psum(down_local.astype(jnp.bfloat16), "seq").astype(jnp.float32),
+        jnp.sum(lax.all_gather(down_local.astype(jnp.bfloat16), "seq"), axis=0).astype(jnp.float32),
         lax.psum(up_query_local.astype(jnp.bfloat16), "seq").astype(jnp.float32),
         lax.psum(up_pair_local.astype(jnp.bfloat16), "seq").astype(jnp.float32),
     )

time: 417 us -> 326 us (0.78)
  the two profiles are of different devices: /device:TPU:41 before, /device:TPU:0 now
where the time goes in v1:
time: 326 us; the launch traced here: 325 us
  blocking collectives  146 us (45%)
  waiting for transfers between devices  50.2 us (15%)
  matrix products  46.5 us (14%)
  other arithmetic  25.1 us (8%)
  starting transfers between devices  24.7 us (8%)
  local copies, waits for them, and re-layouts  17.4 us (5%)
  between operations  14.4 us (4%)
    psum x1, blocking collectives, body(): lax.psum(up_query_local.astype(jnp.bfloat16), 'seq').astype(jnp.float32)  105 us
    ppermute x14, waiting for transfers between devices, from_behind(): return lax.ppermute(value, axis, pairs)  50.1 us
    psum x1, blocking collectives, body(): lax.psum(backward_piece.astype(jnp.bfloat16), 'head').astype(jnp.float32)  41.7 us
    ppermute x14, starting transfers between devices, from_behind(): return lax.ppermute(value, axis, pairs)  24.7 us
    dot_general x4, matrix products, head_block(): jnp.einsum('hqk,kd->qhd', prob_bf16, value_all, preferred_element_type=jn...  14.7 us
    dot_general x4, matrix products, head_block(): jnp.einsum('hqk,qhd->kd', prob_bf16, grad_blk, preferred_element_type=jnp...  9.32 us
    unnamed x35, local copies, waits for them, and re-layouts  7.3 us
    dot_general x4, matrix products, head_block(): jnp.einsum('hqk,qhd->kd', dscore, query_blk, preferred_element_type=jnp.f...  6.94 us
  transfers between devices with their start and end apart: 15, of which 14 were waited for; matrix products, arithmetic and copies ran while one was open for 5% of the time, Pallas kernels for 0%

profile of v1, /device:TPU:0, one launch (start us, length us, event | category | flops | bytes accessed | tf_op | source)
XLA Modules:
  0.0 325.0 jit_solution(13021589301748127633)
XLA Ops:
  14.9 2.0 copy.40
  19.3 5.5 %collective-permute-done.1 = bf16[256,256]{1,0:T(8,128)(2,1)S(1)} collective-permute-done((bf16[256,256]{1,0:T(8,128)(2,1)}, bf16[256,256]{1,0:T(8,128)(2,1)S(1)}, u32[]{:S(2)}, u32[]{:S(2)}) %collective-permute-start.1) | collective-permute-done | bytes 131104 | tf_op jit(solution)/shard_map/ppermute | solution.py:13
  25.4 5.8 %collective-permute-done.2 = bf16[256,256]{1,0:T(8,128)(2,1)S(1)} collective-permute-done((bf16[256,256]{1,0:T(8,128)(2,1)S(1)}, bf16[256,256]{1,0:T(8,128)(2,1)S(1)}, u32[]{:S(2)}, u32[]{:S(2)}) %collective-permute-start.2) | collective-permute-done | bytes 131104 | tf_op jit(solution)/shard_map/ppermute | solution.py:13
  31.9 5.8 %collective-permute-done.3 = bf16[256,256]{1,0:T(8,128)(2,1)S(1)} collective-permute-done((bf16[256,256]{1,0:T(8,128)(2,1)S(1)}, bf16[256,256]{1,0:T(8,128)(2,1)S(1)}, u32[]{:S(2)}, u32[]{:S(2)}) %collective-permute-start.3) | collective-permute-done | bytes 131104 | tf_op jit(solution)/shard_map/ppermute | solution.py:13
  38.4 5.8 %collective-permute-done.4 = bf16[256,256]{1,0:T(8,128)(2,1)S(1)} collective-permute-done((bf16[256,256]{1,0:T(8,128)(2,1)S(1)}, bf16[256,256]{1,0:T(8,128)(2,1)S(1)}, u32[]{:S(2)}, u32[]{:S(2)}) %collective-permute-start.4) | collective-permute-done | bytes 131104 | tf_op jit(solution)/shard_map/ppermute | solution.py:13
  44.9 5.8 %collective-permute-done.5 = bf16[256,256]{1,0:T(8,128)(2,1)S(1)} collective-permute-done((bf16[256,256]{1,0:T(8,128)(2,1)S(1)}, bf16[256,256]{1,0:T(8,128)(2,1)S(1)}, u32[]{:S(2)}, u32[]{:S(2)}) %collective-permute-start.5) | collective-permute-done | bytes 131104 | tf_op jit(solution)/shard_map/ppermute | solution.py:13
  51.4 5.8 %collective-permute-done.6 = bf16[256,256]{1,0:T(8,128)(2,1)S(1)} collective-permute-done((bf16[256,256]{1,0:T(8,128)(2,1)S(1)}, bf16[256,256]{1,0:T(8,128)(2,1)S(1)}, u32[]{:S(2)}, u32[]{:S(2)}) %collective-permute-start.6) | collective-permute-done | bytes 131104 | tf_op jit(solution)/shard_map/ppermute | solution.py:13
  60.3 56.6 %while.15 = (s32[]{:T(128)}, f32[4,256,2,128]{3,1,2,0:T(8,128)S(1)}, f32[4,2048,128]{2,1,0:T(8,128)}, f32[4,2048,128]{2,1,0:T(8,128)}, bf16[4,256,2,128]{3,1,2,0...) while((s32[]{:T(128)}, ...), condition=%wide.region_4.5_spmd.clone, body=%wide.region_0.4_spmd.clone.sunk | while | flops 1634860032 | bytes 71749384 | solution.py:149
  64.1 2.3 fusion.144
  66.6 3.7 %fusion.140 = f32[256,2]{0,1:T(2,128)S(1)} fusion(bf16[2048,128]{0,1:T(8,128)(2,1)} %get-tuple-element.255, bf16[1,256,2,128]{3,1,2,0:T(8,128)(2,1)S(1)} %copy.63, f32[256,2,2048]{2,0,1:T(8,128)} %copy-done.1, f32[2,256]{1,0:T(2,128)} %copy-done.9, pred[256,2048]{1,0:T(8,128)(4,1)S(1)} %fusion.138), kind=kOutput, calls=%fused_computation.27.clone.1 | convolution fusion | flops 272956928 | bytes 5378048 | tf_op jit(solution)/shard_map/while/body/eval_jaxpr/hqk,kd->qhd/dot_general | solution.py:126
  78.3 2.3 fusion.144
  80.7 3.7 %fusion.140 = f32[256,2]{0,1:T(2,128)S(1)} fusion(bf16[2048,128]{0,1:T(8,128)(2,1)} %get-tuple-element.255, bf16[1,256,2,128]{3,1,2,0:T(8,128)(2,1)S(1)} %copy.63, f32[256,2,2048]{2,0,1:T(8,128)} %copy-done.1, f32[2,256]{1,0:T(2,128)} %copy-done.9, pred[256,2048]{1,0:T(8,128)(4,1)S(1)} %fusion.138), kind=kOutput, calls=%fused_computation.27.clone.1 | convolution fusion | flops 272956928 | bytes 5378048 | tf_op jit(solution)/shard_map/while/body/eval_jaxpr/hqk,kd->qhd/dot_general | solution.py:126
  92.4 2.3 fusion.144
  94.9 3.7 %fusion.140 = f32[256,2]{0,1:T(2,128)S(1)} fusion(bf16[2048,128]{0,1:T(8,128)(2,1)} %get-tuple-element.255, bf16[1,256,2,128]{3,1,2,0:T(8,128)(2,1)S(1)} %copy.63, f32[256,2,2048]{2,0,1:T(8,128)} %copy-done.1, f32[2,256]{1,0:T(2,128)} %copy-done.9, pred[256,2048]{1,0:T(8,128)(4,1)S(1)} %fusion.138), kind=kOutput, calls=%fused_computation.27.clone.1 | convolution fusion | flops 272956928 | bytes 5378048 | tf_op jit(solution)/shard_map/while/body/eval_jaxpr/hqk,kd->qhd/dot_general | solution.py:126
  106.6 2.4 fusion.144
  109.1 3.7 %fusion.140 = f32[256,2]{0,1:T(2,128)S(1)} fusion(bf16[2048,128]{0,1:T(8,128)(2,1)} %get-tuple-element.255, bf16[1,256,2,128]{3,1,2,0:T(8,128)(2,1)S(1)} %copy.63, f32[256,2,2048]{2,0,1:T(8,128)} %copy-done.1, f32[2,256]{1,0:T(2,128)} %copy-done.9, pred[256,2048]{1,0:T(8,128)(4,1)S(1)} %fusion.138), kind=kOutput, calls=%fused_computation.27.clone.1 | convolution fusion | flops 272956928 | bytes 5378048 | tf_op jit(solution)/shard_map/while/body/eval_jaxpr/hqk,kd->qhd/dot_general | solution.py:126
  116.9 2.8 reduce_sum.48
  119.8 2.5 reduce_sum.49
  122.4 2.5 collective-permute-done.7
  125.0 4.1 %collective-permute-start.8 = (bf16[2,256,128]{2,1,0:T(8,128)(2,1)S(1)}, bf16[2,256,128]{2,1,0:T(8,128)(2,1)S(1)}, u32[]{:S(2)}, u32[]{:S(2)}) collective-permute-start(bf16[2,256,128]{2,1,0:T(8,128)(2,1)S(1)} %fusion.51), channel_id=1, source_target_pairs={{0,248},{8,0},{16,8},{24,16},{32,24},{40,32},{48,40},{56,48},{64,5... | collective-permute-start | bytes 393224 | tf_op jit(solution)/shard_map/ppermute | solution.py:13
  129.1 2.5 collective-permute-done.8
  131.6 4.1 %collective-permute-start.9 = (bf16[2,256,128]{2,1,0:T(8,128)(2,1)S(1)}, bf16[2,256,128]{2,1,0:T(8,128)(2,1)S(1)}, u32[]{:S(2)}, u32[]{:S(2)}) collective-permute-start(bf16[2,256,128]{2,1,0:T(8,128)(2,1)S(1)} %fusion.55), channel_id=1, source_target_pairs={{0,248},{8,0},{16,8},{24,16},{32,24},{40,32},{48,40},{56,48},{64,5... | collective-permute-start | bytes 393224 | tf_op jit(solution)/shard_map/ppermute | solution.py:13
  135.7 2.5 collective-permute-done.9
  138.2 4.3 %collective-permute-start.10 = (bf16[2,256,128]{2,1,0:T(8,128)(2,1)S(1)}, bf16[2,256,128]{2,1,0:T(8,128)(2,1)S(1)}, u32[]{:S(2)}, u32[]{:S(2)}) collective-permute-start(bf16[2,256,128]{2,1,0:T(8,128)(2,1)S(1)} %fusion.59), channel_id=1, source_target_pairs={{0,248},{8,0},{16,8},{24,16},{32,24},{40,32},{48,40},{56,48},{64,5... | collective-permute-start | bytes 393224 | tf_op jit(solution)/shard_map/ppermute | solution.py:13
  142.8 2.3 collective-permute-done.10
  145.1 4.1 %collective-permute-start.11 = (bf16[2,256,128]{2,1,0:T(8,128)(2,1)S(1)}, bf16[2,256,128]{2,1,0:T(8,128)(2,1)S(1)}, u32[]{:S(2)}, u32[]{:S(2)}) collective-permute-start(bf16[2,256,128]{2,1,0:T(8,128)(2,1)S(1)} %fusion.63), channel_id=1, source_target_pairs={{0,248},{8,0},{16,8},{24,16},{32,24},{40,32},{48,40},{56,48},{64,5... | collective-permute-start | bytes 393224 | tf_op jit(solution)/shard_map/ppermute | solution.py:13
  149.5 2.2 collective-permute-done.11
  151.7 4.1 %collective-permute-start.12 = (bf16[2,256,128]{2,1,0:T(8,128)(2,1)S(1)}, bf16[2,256,128]{2,1,0:T(8,128)(2,1)S(1)}, u32[]{:S(2)}, u32[]{:S(2)}) collective-permute-start(bf16[2,256,128]{2,1,0:T(8,128)(2,1)S(1)} %fusion.67), channel_id=1, source_target_pairs={{0,248},{8,0},{16,8},{24,16},{32,24},{40,32},{48,40},{56,48},{64,5... | collective-permute-start | bytes 393224 | tf_op jit(solution)/shard_map/ppermute | solution.py:13
  158.3 4.1 %collective-permute-start.13 = (bf16[2,256,128]{2,1,0:T(8,128)(2,1)S(1)}, bf16[2,256,128]{2,1,0:T(8,128)(2,1)S(1)}, u32[]{:S(2)}, u32[]{:S(2)}) collective-permute-start(bf16[2,256,128]{2,1,0:T(8,128)(2,1)S(1)} %fusion.45), channel_id=1, source_target_pairs={{0,248},{8,0},{16,8},{24,16},{32,24},{40,32},{48,40},{56,48},{64,5... | collective-permute-start | bytes 393224 | tf_op jit(solution)/shard_map/ppermute | solution.py:13
  162.6 2.3 collective-permute-done.13
  165.8 41.7 %all-reduce.1 = (bf16[256,3,8]{0,2,1:T(8,128)(2,1)S(1)}, bf16[256,3,8]{0,2,1:T(8,128)(2,1)S(1)}) all-reduce(bf16[256,3,8]{0,2,1:T(8,128)(2,1)S(1)} %pad_maximum_fusion.6, bf16[256,3,8]{0,2,1:T(8,128)(2,1)S(1)} %convolution_convert_fusion.1), channel_id=1, replica_groups=mesh['seq'=32,'head'=8] {'head'}, use_global_device_ids=true, to_apply=%region_7.8 | all-reduce | flops 12288 | bytes 49152 | tf_op jit(solution)/shard_map/psum | solution.py:188
  208.7 104.5 %all-reduce = (bf16[8,1024]{1,0:T(8,128)(2,1)S(1)}, bf16[2,8,128]{2,1,0:T(8,128)(2,1)S(1)}) all-reduce(bf16[8,1024]{1,0:T(8,128)(2,1)S(1)} %fusion.36, bf16[2,8,128]{2,1,0:T(8,128)(2,1)S(1)} %fusion.38), channel_id=1, replica_groups=mesh['seq'=32,'head'=8] {'seq'}, use_global_device_ids=true, to_apply=%region_10.11 | all-reduce | flops 10240 | bytes 40960 | tf_op jit(solution)/shard_map/psum | solution.py:203
  (169 shorter events, 59.0 us)
Async XLA Ops:
  7.2 135.3 %copy-start = (bf16[256,1024]{1,0:T(8,128)(2,1)S(1)}, bf16[256,1024]{1,0:T(8,128)(2,1)}, u32[]{:S(2)}) copy-start(bf16[256,1024]{1,0:T(8,128)(2,1)} %param.10) | copy-start | bytes 1572868
  7.2 308.6 %all-gather.3.cloned.1.call-start = ((), (), s32[]{:S(2)}) async-start(), calls=%async_computation | async-start | bytes 1622016 | tf_op jit(solution)/shard_map/all_gather | solution.py:202
  7.2 6.4 %copy-start.15 = (f32[64]{0:T(128)}, f32[64]{0:T(128)S(1)}, u32[]{:S(2)}) copy-start(f32[64]{0:T(128)S(1)} %power_multiply_fusion) | copy-start | bytes 772
  7.3 6.3 %copy-start.13 = (f32[256]{0:T(256)}, f32[256]{0:T(256)S(1)}, u32[]{:S(2)}) copy-start(f32[256]{0:T(256)S(1)} %add_convert_fusion.1) | copy-start | bytes 3076
  10.4 7.4 %collective-permute-start = (bf16[256,256]{1,0:T(8,128)(2,1)S(1)}, bf16[256,256]{1,0:T(8,128)(2,1)}, u32[]{:S(2)}, u32[]{:S(2)}) collective-permute-start(bf16[256,256]{1,0:T(8,128)(2,1)S(1)} %get-tuple-element.134), channel_id=1, source_target_pairs={{0,8},{8,16},{16,24},{24,32},{32,40},{40,48},{48,56},{56,64},{64,7... | collective-permute-start | bytes 393224 | tf_op jit(solution)/shard_map/ppermute | solution.py:13
  10.9 3.9 %copy-start.6 = (f32[256,64]{1,0:T(8,128)}, f32[256,64]{1,0:T(8,128)S(1)}, u32[]{:S(2)}) copy-start(f32[256,64]{1,0:T(8,128)S(1)} %get-tuple-element.150) | copy-start | bytes 196612
  17.7 7.0 %collective-permute-start.1 = (bf16[256,256]{1,0:T(8,128)(2,1)}, bf16[256,256]{1,0:T(8,128)(2,1)S(1)}, u32[]{:S(2)}, u32[]{:S(2)}) collective-permute-start(bf16[256,256]{1,0:T(8,128)(2,1)} %collective-permute-done), channel_id=1, source_target_pairs={{0,8},{8,16},{16,24},{24,32},{32,40},{40,48},{48,56},{56,64},{64,7... | collective-permute-start | bytes 393224 | tf_op jit(solution)/shard_map/ppermute | solution.py:13
  24.8 6.5 %collective-permute-start.2 = (bf16[256,256]{1,0:T(8,128)(2,1)S(1)}, bf16[256,256]{1,0:T(8,128)(2,1)S(1)}, u32[]{:S(2)}, u32[]{:S(2)}) collective-permute-start(bf16[256,256]{1,0:T(8,128)(2,1)S(1)} %collective-permute-done.1), channel_id=1, source_target_pairs={{0,8},{8,16},{16,24},{24,32},{32,40},{40,48},{48,56},{56,64},{64,7... | collective-permute-start | bytes 393224 | tf_op jit(solution)/shard_map/ppermute | solution.py:13
  31.3 6.5 %collective-permute-start.3 = (bf16[256,256]{1,0:T(8,128)(2,1)S(1)}, bf16[256,256]{1,0:T(8,128)(2,1)S(1)}, u32[]{:S(2)}, u32[]{:S(2)}) collective-permute-start(bf16[256,256]{1,0:T(8,128)(2,1)S(1)} %collective-permute-done.2), channel_id=1, source_target_pairs={{0,8},{8,16},{16,24},{24,32},{32,40},{40,48},{48,56},{56,64},{64,7... | collective-permute-start | bytes 393224 | tf_op jit(solution)/shard_map/ppermute | solution.py:13
  37.8 6.5 %collective-permute-start.4 = (bf16[256,256]{1,0:T(8,128)(2,1)S(1)}, bf16[256,256]{1,0:T(8,128)(2,1)S(1)}, u32[]{:S(2)}, u32[]{:S(2)}) collective-permute-start(bf16[256,256]{1,0:T(8,128)(2,1)S(1)} %collective-permute-done.3), channel_id=1, source_target_pairs={{0,8},{8,16},{16,24},{24,32},{32,40},{40,48},{48,56},{56,64},{64,7... | collective-permute-start | bytes 393224 | tf_op jit(solution)/shard_map/ppermute | solution.py:13
  44.3 6.5 %collective-permute-start.5 = (bf16[256,256]{1,0:T(8,128)(2,1)S(1)}, bf16[256,256]{1,0:T(8,128)(2,1)S(1)}, u32[]{:S(2)}, u32[]{:S(2)}) collective-permute-start(bf16[256,256]{1,0:T(8,128)(2,1)S(1)} %collective-permute-done.4), channel_id=1, source_target_pairs={{0,8},{8,16},{16,24},{24,32},{32,40},{40,48},{48,56},{56,64},{64,7... | collective-permute-start | bytes 393224 | tf_op jit(solution)/shard_map/ppermute | solution.py:13
  50.8 6.5 %collective-permute-start.6 = (bf16[256,256]{1,0:T(8,128)(2,1)S(1)}, bf16[256,256]{1,0:T(8,128)(2,1)S(1)}, u32[]{:S(2)}, u32[]{:S(2)}) collective-permute-start(bf16[256,256]{1,0:T(8,128)(2,1)S(1)} %collective-permute-done.5), channel_id=1, source_target_pairs={{0,8},{8,16},{16,24},{24,32},{32,40},{40,48},{48,56},{56,64},{64,7... | collective-permute-start | bytes 393224 | tf_op jit(solution)/shard_map/ppermute | solution.py:13
  66.6 3.7 %copy-start.8 = (bf16[2048,128]{0,1:T(8,128)(2,1)S(1)}, bf16[2048,128]{0,1:T(8,128)(2,1)}, u32[]{:S(2)}) copy-start(bf16[2048,128]{0,1:T(8,128)(2,1)} %get-tuple-element.255) | copy-start | bytes 1572868 | tf_op jit(solution)/shard_map/while
  66.6 3.7 %copy-start.10 = (f32[2,256]{1,0:T(2,128)S(1)}, f32[2,256]{1,0:T(2,128)}, u32[]{:S(2)}) copy-start(f32[2,256]{1,0:T(2,128)} %copy-done.9) | copy-start | bytes 6148 | tf_op jit(solution)/shard_map/while
  80.7 3.7 %copy-start.8 = (bf16[2048,128]{0,1:T(8,128)(2,1)S(1)}, bf16[2048,128]{0,1:T(8,128)(2,1)}, u32[]{:S(2)}) copy-start(bf16[2048,128]{0,1:T(8,128)(2,1)} %get-tuple-element.255) | copy-start | bytes 1572868 | tf_op jit(solution)/shard_map/while
  94.8 3.7 %copy-start.8 = (bf16[2048,128]{0,1:T(8,128)(2,1)S(1)}, bf16[2048,128]{0,1:T(8,128)(2,1)}, u32[]{:S(2)}) copy-start(bf16[2048,128]{0,1:T(8,128)(2,1)} %get-tuple-element.255) | copy-start | bytes 1572868 | tf_op jit(solution)/shard_map/while
  109.1 3.7 %copy-start.8 = (bf16[2048,128]{0,1:T(8,128)(2,1)S(1)}, bf16[2048,128]{0,1:T(8,128)(2,1)}, u32[]{:S(2)}) copy-start(bf16[2048,128]{0,1:T(8,128)(2,1)} %get-tuple-element.255) | copy-start | bytes 1572868 | tf_op jit(solution)/shard_map/while
  122.3 20.2 %copy-start.11 = (bf16[3,8,1024]{2,1,0:T(8,128)(2,1)S(1)}, bf16[3,8,1024]{2,1,0:T(8,128)(2,1)}, u32[]{:S(2)}) copy-start(bf16[3,8,1024]{2,1,0:T(8,128)(2,1)} %param.15) | copy-start | bytes 147460
  122.4 2.6 collective-permute-start.7
  125.0 24.1 %copy-start.5 = (f32[4,256,2,128]{3,1,2,0:T(8,128)S(1)}, f32[4,256,2,128]{3,1,2,0:T(8,128)}, u32[]{:S(2)}) copy-start(f32[4,256,2,128]{3,1,2,0:T(8,128)} %copy-done.4) | copy-start | bytes 3145732
  125.0 6.6 %collective-permute-start.8 = (bf16[2,256,128]{2,1,0:T(8,128)(2,1)S(1)}, bf16[2,256,128]{2,1,0:T(8,128)(2,1)S(1)}, u32[]{:S(2)}, u32[]{:S(2)}) collective-permute-start(bf16[2,256,128]{2,1,0:T(8,128)(2,1)S(1)} %fusion.51), channel_id=1, source_target_pairs={{0,248},{8,0},{16,8},{24,16},{32,24},{40,32},{48,40},{56,48},{64,5... | collective-permute-start | bytes 393224 | tf_op jit(solution)/shard_map/ppermute | solution.py:13
  131.6 6.6 %collective-permute-start.9 = (bf16[2,256,128]{2,1,0:T(8,128)(2,1)S(1)}, bf16[2,256,128]{2,1,0:T(8,128)(2,1)S(1)}, u32[]{:S(2)}, u32[]{:S(2)}) collective-permute-start(bf16[2,256,128]{2,1,0:T(8,128)(2,1)S(1)} %fusion.55), channel_id=1, source_target_pairs={{0,248},{8,0},{16,8},{24,16},{32,24},{40,32},{48,40},{56,48},{64,5... | collective-permute-start | bytes 393224 | tf_op jit(solution)/shard_map/ppermute | solution.py:13
  138.2 6.8 %collective-permute-start.10 = (bf16[2,256,128]{2,1,0:T(8,128)(2,1)S(1)}, bf16[2,256,128]{2,1,0:T(8,128)(2,1)S(1)}, u32[]{:S(2)}, u32[]{:S(2)}) collective-permute-start(bf16[2,256,128]{2,1,0:T(8,128)(2,1)S(1)} %fusion.59), channel_id=1, source_target_pairs={{0,248},{8,0},{16,8},{24,16},{32,24},{40,32},{48,40},{56,48},{64,5... | collective-permute-start | bytes 393224 | tf_op jit(solution)/shard_map/ppermute | solution.py:13
  142.8 13.0 %copy-start.7 = (f32[256,64]{1,0:T(8,128)S(1)}, f32[256,64]{1,0:T(8,128)}, u32[]{:S(2)}) copy-start(f32[256,64]{1,0:T(8,128)} %copy-done.6) | copy-start | bytes 196612
  145.1 6.6 %collective-permute-start.11 = (bf16[2,256,128]{2,1,0:T(8,128)(2,1)S(1)}, bf16[2,256,128]{2,1,0:T(8,128)(2,1)S(1)}, u32[]{:S(2)}, u32[]{:S(2)}) collective-permute-start(bf16[2,256,128]{2,1,0:T(8,128)(2,1)S(1)} %fusion.63), channel_id=1, source_target_pairs={{0,248},{8,0},{16,8},{24,16},{32,24},{40,32},{48,40},{56,48},{64,5... | collective-permute-start | bytes 393224 | tf_op jit(solution)/shard_map/ppermute | solution.py:13
  151.7 6.6 %collective-permute-start.12 = (bf16[2,256,128]{2,1,0:T(8,128)(2,1)S(1)}, bf16[2,256,128]{2,1,0:T(8,128)(2,1)S(1)}, u32[]{:S(2)}, u32[]{:S(2)}) collective-permute-start(bf16[2,256,128]{2,1,0:T(8,128)(2,1)S(1)} %fusion.67), channel_id=1, source_target_pairs={{0,248},{8,0},{16,8},{24,16},{32,24},{40,32},{48,40},{56,48},{64,5... | collective-permute-start | bytes 393224 | tf_op jit(solution)/shard_map/ppermute | solution.py:13
  155.7 6.6 %copy-start.12 = (bf16[8,1024]{1,0:T(8,128)(2,1)S(1)}, bf16[8,1024]{1,0:T(8,128)(2,1)}, u32[]{:S(2)}) copy-start(bf16[8,1024]{1,0:T(8,128)(2,1)} %param.16) | copy-start | bytes 49156
  157.1 7.8 %copy-start.14 = (f32[256]{0:T(256)S(1)}, f32[256]{0:T(256)}, u32[]{:S(2)}) copy-start(f32[256]{0:T(256)} %copy-done.13) | copy-start | bytes 3076
  157.1 7.8 %copy-start.16 = (f32[64]{0:T(128)S(1)}, f32[64]{0:T(128)}, u32[]{:S(2)}) copy-start(f32[64]{0:T(128)} %copy-done.15) | copy-start | bytes 772
  157.1 8.4 %copy-start.17 = (bf16[2,8,128]{2,1,0:T(8,128)(2,1)S(1)}, bf16[2,8,128]{2,1,0:T(8,128)(2,1)}, u32[]{:S(2)}) copy-start(bf16[2,8,128]{2,1,0:T(8,128)(2,1)} %param.17) | copy-start | bytes 12292
  157.5 158.3 %copy-start.3 = (bf16[32,8,8,128]{3,1,2,0:T(8,128)(2,1)}, bf16[32,8,8,128]{3,1,2,0:T(8,128)(2,1)S(1)}, u32[]{:S(2)}) copy-start(bf16[32,8,8,128]{3,1,2,0:T(8,128)(2,1)S(1)} %copy.61) | copy-start | bytes 1572868
  158.3 6.6 %collective-permute-start.13 = (bf16[2,256,128]{2,1,0:T(8,128)(2,1)S(1)}, bf16[2,256,128]{2,1,0:T(8,128)(2,1)S(1)}, u32[]{:S(2)}, u32[]{:S(2)}) collective-permute-start(bf16[2,256,128]{2,1,0:T(8,128)(2,1)S(1)} %fusion.45), channel_id=1, source_target_pairs={{0,248},{8,0},{16,8},{24,16},{32,24},{40,32},{48,40},{56,48},{64,5... | collective-permute-start | bytes 393224 | tf_op jit(solution)/shard_map/ppermute | solution.py:13
  (16 other events, 42.7 us)
Sparse Core Ops, SparseCore 0:
  208.4 59.6 all-gather.2
